TPU v7x, 256 devices: a whole 4x4x8 slice. The times are simulated.
256 devices in a mesh: section: 16 (over z_hi, y), dp: 8 (over x, core), spatial: 2 (over z_lo).
Axes of the slice: x: 4, y: 4, z: 8 (z_hi: 4, z_lo: 2; z = z_hi * 2 + z_lo), core: 2. Of those that a mesh axis runs over, the one named last changes fastest.
Arguments:
- inbox: bfloat16 [16, 4, 8, 256, 4, 128], P('section', None, 'dp', None, 'spatial'), may hold values from -6 to 6
- fresh: bfloat16 [3, 4, 8, 256, 4, 128], P(None, None, 'dp', None, 'spatial'), may hold values from -6 to 6
- params: float32 [16, 2, 9, 256, 256], P('section', None, None, ('dp', 'spatial')), may hold values from -6 to 6
- moments: float32 [16, 2, 9, 256, 256], P('section', None, None, ('dp', 'spatial')), may hold values from -3 to 3
Outputs:
- outbox: bfloat16 [16, 4, 8, 256, 4, 128], P('section', None, 'dp', None, 'spatial')
- params_out: float32 [16, 2, 9, 256, 256], P('section', None, None, ('dp', 'spatial'))
- moments_out: float32 [16, 2, 9, 256, 256], P('section', None, None, ('dp', 'spatial'))
All inputs are finite; a program needn't handle non-finite values.
Results may differ from a plain program's by a relative error of at most 0.024.
Values may be sent and summed in bfloat16 or wider, within the bound.
A program may use at most 64 MiB of HBM per device.

v0:
```python
import math

import jax
import jax.numpy as jnp
from jax import lax
from jax.experimental import pallas as pl
from jax.experimental.pallas import tpu as pltpu
from jax.sharding import PartitionSpec as P

MESH = pl.DeviceIdType.MESH
LEARN_RATE = 0.05
MOMENTUM = 0.9
F, G = 0, 1
bf16, f32 = jnp.bfloat16, jnp.float32


def wait_for(ref, sem):
    pltpu.make_async_copy(ref, ref, sem).wait()


def slope(v):
    s = jax.nn.sigmoid(v)
    return s * (1.0 + v * (1.0 - s))


def kernel(inbox, fresh, par_in, mom_in, out, par, mom,
           msg, obuf, abuf, halo, V, gp, crecv, mrecv, fs, zrecv, kbuf,
           ag_s, ag_r, rs_s, rs_r, m_s, m_r, w_s, h_s, h_r, o_s, o_r):
    ticks = msg.shape[0]
    C = msg.shape[3]
    scale = 1.0 / math.sqrt(9 * C)
    sec = lax.axis_index("section")
    n_sec = lax.axis_size("section")
    dp = lax.axis_index("dp")
    z = lax.axis_index("spatial")
    x = dp // 2
    c = lax.rem(dp, 2)
    xp, xm, x2 = lax.rem(x + 1, 4), lax.rem(x + 3, 4), lax.rem(x + 2, 4)
    XP = {"dp": lax.rem(dp + 2, 8)}
    XM = {"dp": lax.rem(dp + 6, 8)}
    CP = {"dp": dp + 1 - 2 * c}
    ZP = {"spatial": 1 - z}
    DG = {"dp": dp + 1 - 2 * c, "spatial": 1 - z}
    UP = {"section": lax.rem(sec + 1, n_sec)}
    DOWN = {"section": lax.rem(sec + n_sec - 1, n_sec)}
    top = sec == n_sec - 1
    stays = c == z

    def rc(src, dst, ss, rs, dev):
        return pltpu.make_async_remote_copy(
            src_ref=src, dst_ref=dst, send_sem=ss, recv_sem=rs,
            device_id=dev, device_id_type=MESH)

    barrier = pltpu.get_barrier_semaphore()
    for dev in (XP, XM, CP, ZP, DG, UP, DOWN):
        pl.semaphore_signal(barrier, inc=1, device_id=dev, device_id_type=MESH)
    pl.semaphore_wait(barrier, 7)

    def row(xx, cc, zz):
        return pl.multiple_of(64 * xx + 32 * cc + 16 * zz, 16)

    def kpart(k, t, xx, zz):
        return kbuf.at[k, t, :, pl.ds(row(xx, c, zz), 16), :]

    def ag(k, t, i, xx, zz, dev):
        part = kpart(k, t, xx, zz)
        return rc(part, part, ag_s.at[k, t, i], ag_r.at[k, t, i], dev)

    def ag_own(k, t):
        return [ag(k, t, 1 + z, x, z, XP), ag(k, t, 3 + z, x, z, XM),
                ag(k, t, 0, x, z, ZP), ag(k, t, 7 + z, x, z, CP)]

    def ag_pair(k, t):
        return [ag(k, t, 2 - z, x, 1 - z, XP), ag(k, t, 4 - z, x, 1 - z, XM),
                ag(k, t, 8 - z, x, 1 - z, CP)]

    def ag_wait(k, t, i):
        wait_for(kpart(k, t, x, z), ag_r.at[k, t, i])

    def gather_0(k, t):
        kbuf[k, t, :, pl.ds(row(x, c, z), 16), :] = (par[k] * scale).astype(bf16)
        for d in ag_own(k, t):
            d.start()

    def gather_1(k, t):
        ag_wait(k, t, 0)
        for d in ag_pair(k, t):
            d.start()
        ag_wait(k, t, 1)
        ag(k, t, 5, xm, 0, XP).start()
        ag(k, t, 9, xm, 0, CP).start()
        ag_wait(k, t, 4)
        ag(k, t, 6, xp, 1, XM).start()
        ag(k, t, 12, xp, 1, CP).start()
        ag_wait(k, t, 2)
        ag(k, t, 10, xm, 1, CP).start()
        ag_wait(k, t, 3)
        ag(k, t, 11, xp, 0, CP).start()

    def gather_2(k, t):
        ag_wait(k, t, 5)
        ag(k, t, 13, x2, 0, CP).start()
        ag_wait(k, t, 6)
        ag(k, t, 14, x2, 1, CP).start()

    def gather_3(k, t):
        for i in range(7, 15):
            ag_wait(k, t, i)

    def gather_sent(k, t):
        for i in range(15):
            wait_for(kpart(k, t, x, z), ag_s.at[k, t, i])

    def gpart(k, t, xx, zz):
        return gp.at[k, t, :, pl.ds(row(xx, c, zz), 16), :]

    order = (x2, xp, xm, x)

    def reduce_0(k, t):
        for j in range(4):
            rc(gp.at[k, t, :, pl.ds(row(order[j], 1 - c, 0), 32), :],
               crecv.at[k, t, :, pl.ds(pl.multiple_of(32 * order[j], 32), 32), :],
               rs_s.at[k, t, j], rs_r.at[k, t, j], CP).start()

    def to(k, t, i, m, xx, zz, dev):
        return rc(gpart(k, t, xx, zz), mrecv.at[k, t, m], rs_s.at[k, t, i], rs_r.at[k, t, i], dev)

    def reduce_1(k, t):
        for j in range(4):
            other = crecv.at[k, t, :, pl.ds(pl.multiple_of(32 * order[j], 32), 32), :]
            wait_for(other, rs_r.at[k, t, j])
            mine = gp.at[k, t, :, pl.ds(row(order[j], c, 0), 32), :]
            mine[...] = (mine[...].astype(f32) + other[...].astype(f32)).astype(bf16)
            if j == 0:
                to(k, t, 4, 0, x2, 0, XP).start()
                to(k, t, 7, 3, x2, 1, XM).start()
            if j == 1:
                to(k, t, 5, 1, xp, 1, XP).start()
            if j == 2:
                to(k, t, 8, 4, xm, 0, XM).start()

    def reduce_2(k, t):
        for m, i, xx, zz, dev in ((0, 4, xp, 0, XP), (3, 7, xm, 1, XM)):
            got = mrecv.at[k, t, m]
            wait_for(got, rs_r.at[k, t, i])
            mine = gpart(k, t, xx, zz)
            mine[...] = (mine[...].astype(f32) + got[...].astype(f32)).astype(bf16)
            to(k, t, i + 2, m + 2, xx, zz, dev).start()

    def reduce_3(k, t):
        for i, m in ((5, 1), (8, 4), (6, 2), (9, 5)):
            wait_for(mrecv.at[k, t, m], rs_r.at[k, t, i])

        def total(zz):
            return (gpart(k, t, x, zz)[...].astype(f32)
                    + mrecv[k, t, 2 - zz].astype(f32) + mrecv[k, t, 4 + zz].astype(f32))

        theirs = gpart(k, t, x, 1 - z)
        theirs[...] = total(1 - z).astype(bf16)
        rc(theirs, zrecv.at[k, t], rs_s.at[k, t, 10], rs_r.at[k, t, 10], ZP).start()
        fs[k] = total(z)

    def reduce_4(k, t):
        wait_for(zrecv.at[k, t], rs_r.at[k, t, 10])
        grad = fs[k] + zrecv[k, t].astype(f32)
        mom[k] = MOMENTUM * mom[k] + scale * grad
        par[k] = par[k] - LEARN_RATE * mom[k]

    def reduce_sent(k, t):
        for j in range(4):
            wait_for(crecv.at[k, t, :, pl.ds(0, 32), :], rs_s.at[k, t, j])
        for i in range(4, 11):
            wait_for(zrecv.at[k, t], rs_s.at[k, t, i])

    def swap(src, dst, ss, rs):
        @pl.when(stays)
        def _():
            pltpu.make_async_copy(src, dst, rs).start()

        @pl.when(jnp.logical_not(stays))
        def _():
            rc(src, dst, ss, rs, DG).start()

    def send_down(t, m):
        return rc(obuf.at[t, m], msg.at[t + 1, m], m_s.at[t + 1, m], m_r.at[t + 1, m], DOWN)

    def emit(t, members):
        @pl.when(jnp.logical_and(t < ticks - 1, sec > 0))
        def _():
            for m in members:
                send_down(t, m).start()

        @pl.when(t == ticks - 1)
        def _():
            for m in members:
                swap(obuf.at[ticks - 1, m], out.at[m], o_s.at[m], o_r.at[m])

    w = lax.broadcasted_iota(jnp.int32, (128, C), 0)

    def put(f, r, v):
        V[f, 1, r] = v.astype(bf16)
        V[f, 0, r] = jnp.where(w == 0, 0.0, pltpu.roll(v, 1, 0)).astype(bf16)
        V[f, 2, r] = jnp.where(w == 127, 0.0, pltpu.roll(v, 127, 0)).astype(bf16)

    def window(f, a, b):
        return V[f, b, a:a + 2].reshape(256, C)

    hoff = pl.multiple_of(128 * (1 - c), 128)
    hrow = 3 * (1 - c)

    def halo_send(t, f, src):
        rc(src.at[pl.ds(hoff, 128), :], halo.at[t, f], h_s.at[t, f], h_r.at[t, f], CP).start()

    def halo_put(t, f):
        wait_for(halo.at[t, f], h_r.at[t, f])
        put(f, hrow, halo[t, f].astype(f32))

    def kernel_grads(k, t, fa, g):
        gt = g.T
        for a in range(3):
            for b in range(3):
                gp[k, t, 3 * a + b] = jnp.dot(
                    gt, window(fa, a, b), preferred_element_type=f32).astype(bf16)

    def conv(k, t, f):
        acc = jnp.zeros((256, C), f32)
        for a in range(3):
            for b in range(3):
                acc = acc + lax.dot_general(
                    window(f, a, b), kbuf[k, t, 3 * a + b], (((1,), (1,)), ((), ())),
                    preferred_element_type=f32)
        return acc

    def conv_flip(k, t, f):
        acc = jnp.zeros((256, C), f32)
        for a in range(3):
            for b in range(3):
                acc = acc + jnp.dot(
                    window(f, 2 - a, 2 - b), kbuf[k, t, 3 * a + b], preferred_element_type=f32)
        return acc

    par[...] = par_in[...]
    mom[...] = mom_in[...]
    gather_0(G, 0)
    for m in (3, 0, 1, 2):
        swap(inbox.at[m], msg.at[0, m], w_s.at[0, m], m_r.at[0, m])
    gather_0(F, 0)

    @pl.when(top)
    def _():
        for t in range(ticks - 1):
            for m in range(4):
                swap(fresh.at[t, m], msg.at[t + 1, m], w_s.at[t + 1, m], m_r.at[t + 1, m])

    V[:, :, 3 * c] = jnp.zeros((4, 3, 128, C), bf16)

    def tick(t, carry):
        wait_for(msg.at[t, 3], m_r.at[t, 3])
        halo_send(t, 1, msg.at[t, 3])
        wait_for(msg.at[t, 0], m_r.at[t, 0])
        for r in range(2):
            v = msg[t, 0, 128 * r:128 * r + 128].astype(f32)
            abuf[t, 0, 128 * r:128 * r + 128] = jax.nn.silu(v).astype(bf16)
        halo_send(t, 0, abuf.at[t, 0])
        gather_1(G, t)

        @pl.when(t > 0)
        def _():
            reduce_4(F, t - 1)
            gather_0(F, t)

        for r in range(2):
            put(0, 1 + r, abuf[t, 0, 128 * r:128 * r + 128].astype(f32))
            put(1, 1 + r, msg[t, 3, 128 * r:128 * r + 128].astype(f32))
        halo_put(t, 1)
        halo_put(t, 0)
        kernel_grads(G, t, 0, msg[t, 3])
        reduce_0(G, t)
        gather_1(F, t)
        reduce_1(G, t)
        gather_2(G, t)
        gather_3(G, t)

        wait_for(msg.at[t, 1], m_r.at[t, 1])
        prev_two = (msg[t, 1].astype(f32) - conv(G, t, 0)).astype(bf16)
        obuf[t, 1] = prev_two
        abuf[t, 1] = jax.nn.silu(prev_two.astype(f32)).astype(bf16)
        halo_send(t, 2, abuf.at[t, 1])
        wait_for(msg.at[t, 2], m_r.at[t, 2])
        back_one = (msg[t, 2].astype(f32)
                    + slope(msg[t, 0].astype(f32)) * conv_flip(G, t, 1)).astype(bf16)
        obuf[t, 2] = back_one
        halo_send(t, 3, obuf.at[t, 2])
        emit(t, (1, 2))
        gather_2(F, t)
        reduce_2(G, t)
        for r in range(2):
            put(2, 1 + r, abuf[t, 1, 128 * r:128 * r + 128].astype(f32))
            put(3, 1 + r, obuf[t, 2, 128 * r:128 * r + 128].astype(f32))
        halo_put(t, 2)
        halo_put(t, 3)
        kernel_grads(F, t, 2, obuf[t, 2])
        reduce_0(F, t)
        gather_3(F, t)
        obuf[t, 0] = (msg[t, 0].astype(f32) - conv(F, t, 2)).astype(bf16)
        obuf[t, 3] = (msg[t, 3].astype(f32)
                      + slope(obuf[t, 1].astype(f32)) * conv_flip(F, t, 3)).astype(bf16)
        emit(t, (3, 0))
        reduce_1(F, t)
        reduce_3(G, t)
        reduce_2(F, t)
        reduce_4(G, t)

        @pl.when(t < ticks - 1)
        def _():
            gather_0(G, t + 1)

        reduce_3(F, t)
        gather_sent(G, t)
        gather_sent(F, t)
        reduce_sent(G, t)
        for f in range(4):
            wait_for(halo.at[t, f], h_s.at[t, f])
        return carry

    lax.fori_loop(0, ticks, tick, 0)
    reduce_4(F, ticks - 1)
    for t in range(ticks):
        reduce_sent(F, t)
    for m in range(4):
        wait_for(out.at[m], o_r.at[m])

    @pl.when(jnp.logical_not(stays))
    def _():
        for m in range(4):
            wait_for(out.at[m], o_s.at[m])
            wait_for(out.at[m], w_s.at[0, m])

    @pl.when(jnp.logical_and(top, jnp.logical_not(stays)))
    def _():
        for t in range(1, ticks):
            for m in range(4):
                wait_for(out.at[m], w_s.at[t, m])

    @pl.when(sec > 0)
    def _():
        for t in range(1, ticks):
            for m in range(4):
                wait_for(out.at[m], m_s.at[t, m])


def local(inbox, fresh, params, moments):
    T = fresh.shape[0] + 1
    C = inbox.shape[3]
    cells = inbox.shape[4] * inbox.shape[5]
    mine = inbox[0, :, 0].transpose(0, 2, 3, 1).reshape(4, cells, C)
    later = fresh[:, :, 0].transpose(0, 1, 3, 4, 2).reshape(T - 1, 4, cells, C)
    shard = params.shape[1:]
    vmem = pl.BlockSpec(memory_space=pltpu.VMEM)
    dma = pltpu.SemaphoreType.DMA
    out, par, mom = pl.pallas_call(
        kernel,
        out_shape=(jax.ShapeDtypeStruct((4, cells, C), bf16),
                   jax.ShapeDtypeStruct(shard, f32), jax.ShapeDtypeStruct(shard, f32)),
        in_specs=[vmem] * 4,
        out_specs=(vmem,) * 3,
        scratch_shapes=[
            pltpu.VMEM((T, 4, cells, C), bf16),
            pltpu.VMEM((T, 4, cells, C), bf16),
            pltpu.VMEM((T, 2, cells, C), bf16),
            pltpu.VMEM((T, 4, 128, C), bf16),
            pltpu.VMEM((4, 3, 4, 128, C), bf16),
            pltpu.VMEM((2, T, 9, C, C), bf16),
            pltpu.VMEM((2, T, 9, C // 2, C), bf16),
            pltpu.VMEM((2, T, 6, 9, 16, C), bf16),
            pltpu.VMEM((2, 9, 16, C), f32),
            pltpu.VMEM((2, T, 9, 16, C), bf16),
            pltpu.VMEM((2, T, 9, C, C), bf16),
            dma((2, T, 15)), dma((2, T, 15)),
            dma((2, T, 11)), dma((2, T, 11)),
            dma((T, 4)), dma((T, 4)), dma((T, 4)),
            dma((T, 4)), dma((T, 4)),
            dma((4,)), dma((4,)),
        ],
        compiler_params=pltpu.CompilerParams(
            collective_id=0, has_side_effects=True, vmem_limit_bytes=60 << 20),
        cost_estimate=pl.CostEstimate(
            flops=T * 6 * 9 * 2 * C * C * cells, bytes_accessed=1 << 22, transcendentals=0),
        name="relay",
    )(mine, later, params[0], moments[0])
    outbox = out.reshape(4, *inbox.shape[4:], C).transpose(0, 3, 1, 2)[None, :, None]
    return (outbox, par[None], mom[None])


def solution(mesh):
    cells = P("section", None, "dp", None, "spatial", None)
    shards = P("section", None, None, ("dp", "spatial"), None)
    return jax.shard_map(
        local,
        mesh=mesh,
        in_specs=(cells, P(None, None, "dp", None, "spatial", None), shards, shards),
        out_specs=(cells, shards, shards),
        check_vma=False,
    )
```

profile of v0, /device:TPU:88, one launch (start us, length us, event | category | flops | bytes accessed | tf_op | source)
XLA Modules:
  0.0 188.0 jit_solution(376973606024848856)
XLA Ops:
  0.6 2.0 %copy.7 = bf16[4,2,128,256]{3,2,1,0:T(8,128)(2,1)} copy(bf16[4,2,128,256]{2,1,3,0:T(2,128)(2,1)} %bitcast.18) | data formatting | bytes 1048576 | tf_op jit(solution)/shard_map/transpose | solution.py:356
  2.6 4.8 %copy.8 = bf16[3,4,2,128,256]{4,3,2,1,0:T(8,128)(2,1)} copy(bf16[3,4,2,128,256]{3,2,4,1,0:T(2,128)(2,1)} %bitcast.16) | data formatting | bytes 3145728 | tf_op jit(solution)/shard_map/transpose | solution.py:357
  7.4 176.1 %relay.1 = (bf16[4,256,256]{2,1,0:T(8,128)(2,1)}, f32[2,9,16,256]{3,2,1,0:T(8,128)}, f32[2,9,16,256]{3,2,1,0:T(8,128)}) custom-call(bf16[4,256,256]{2,1,0:T(8,128)(2,1)} %bitcast.21, bf16[3,4,256,256]{3,2,1,0:T(8,128)(2,1)} %bitcast.17, f32[2,9,16,256]{3,2,1,0:T(8,128)} %bitcast.24, f32[2,9,16,256]{3,2,1,0:T(8,128)} %bitcast.25), custom_call_target="tpu_custom_call" | custom-call | flops 7247757312 | bytes 4194304 | tf_op jit(solution)/shard_map/relay/pallas_call | solution.py:361
  183.5 0.0 copy-start
  183.5 2.0 %copy.9 = bf16[4,2,128,256]{2,1,3,0:T(2,128)(2,1)} copy(bf16[4,2,128,256]{3,2,1,0:T(8,128)(2,1)} %bitcast.20) | data formatting | bytes 1048576 | tf_op jit(solution)/shard_map/reshape | solution.py:391
  185.6 1.7 copy.12
  187.3 0.0 copy-done
  187.3 0.7 copy.13
Async XLA Ops:
  183.5 3.8 %copy-start = (f32[2,9,16,256]{3,2,1,0:T(8,128)S(1)}, f32[2,9,16,256]{3,2,1,0:T(8,128)}, u32[]{:S(2)}) copy-start(f32[2,9,16,256]{3,2,1,0:T(8,128)} %get-tuple-element.8) | copy-start | bytes 884740
where the time goes:
time: 188 us
  Pallas kernels  176 us (94%)
  local copies, waits for them, and re-layouts  11.3 us (6%)
    pallas_call x1, Pallas kernels, local(): pl.pallas_call(kernel, out_shape=(jax.ShapeDtypeStruct((4, cells, C), bf1...  176 us
    transpose x1, local copies, waits for them, and re-layouts, local(): later = fresh[:, :, 0].transpose(0, 1, 3, 4, 2).reshape(T - 1, 4, cells, C)  4.84 us

commit v1 on v0

--- a/solution.py
+++ b/solution.py
@@ -24,8 +24,8 @@
 
 
 def kernel(inbox, fresh, par_in, mom_in, out, par, mom,
-           msg, obuf, abuf, halo, V, gp, crecv, mrecv, fs, zrecv, kbuf,
-           ag_s, ag_r, rs_s, rs_r, m_s, m_r, w_s, h_s, h_r, o_s, o_r):
+           msg, obuf, abuf, rbuf, halo, V, gp, crecv, mrecv, fs, zrecv, kbuf,
+           ag_s, ag_r, rs_s, rs_r, m_s, m_r, w_s, r_s, r_r, h_s, h_r, o_s, o_r):
     ticks = msg.shape[0]
     C = msg.shape[3]
     scale = 1.0 / math.sqrt(9 * C)
@@ -41,8 +41,11 @@
     CP = {"dp": dp + 1 - 2 * c}
     ZP = {"spatial": 1 - z}
     DG = {"dp": dp + 1 - 2 * c, "spatial": 1 - z}
-    UP = {"section": lax.rem(sec + 1, n_sec)}
-    DOWN = {"section": lax.rem(sec + n_sec - 1, n_sec)}
+    def at(offset):
+        return {"section": lax.rem(sec + n_sec + offset, n_sec)}
+
+    around = jnp.logical_and(lax.rem(sec, 4) == 0, sec > 0)
+    passes = jnp.logical_and(lax.rem(sec, 4) == 3, sec > 3)
     top = sec == n_sec - 1
     stays = c == z
 
@@ -52,9 +55,9 @@
             device_id=dev, device_id_type=MESH)
 
     barrier = pltpu.get_barrier_semaphore()
-    for dev in (XP, XM, CP, ZP, DG, UP, DOWN):
+    for dev in (XP, XM, CP, ZP, DG, at(1), at(-1), at(3), at(-3), at(4), at(-4)):
         pl.semaphore_signal(barrier, inc=1, device_id=dev, device_id_type=MESH)
-    pl.semaphore_wait(barrier, 7)
+    pl.semaphore_wait(barrier, 11)
 
     def row(xx, cc, zz):
         return pl.multiple_of(64 * xx + 32 * cc + 16 * zz, 16)
@@ -86,6 +89,8 @@
         ag_wait(k, t, 0)
         for d in ag_pair(k, t):
             d.start()
+
+    def gather_2(k, t):
         ag_wait(k, t, 1)
         ag(k, t, 5, xm, 0, XP).start()
         ag(k, t, 9, xm, 0, CP).start()
@@ -97,13 +102,13 @@
         ag_wait(k, t, 3)
         ag(k, t, 11, xp, 0, CP).start()
 
-    def gather_2(k, t):
+    def gather_3(k, t):
         ag_wait(k, t, 5)
         ag(k, t, 13, x2, 0, CP).start()
         ag_wait(k, t, 6)
         ag(k, t, 14, x2, 1, CP).start()
 
-    def gather_3(k, t):
+    def gather_4(k, t):
         for i in range(7, 15):
             ag_wait(k, t, i)
 
@@ -182,18 +187,53 @@
             rc(src, dst, ss, rs, DG).start()
 
     def send_down(t, m):
-        return rc(obuf.at[t, m], msg.at[t + 1, m], m_s.at[t + 1, m], m_r.at[t + 1, m], DOWN)
-
-    def emit(t, members):
-        @pl.when(jnp.logical_and(t < ticks - 1, sec > 0))
-        def _():
-            for m in members:
+        return rc(obuf.at[t, m], msg.at[t + 1, m], m_s.at[t + 1, m], m_r.at[t + 1, m], at(-1))
+
+    def send_around(t, m):
+        return rc(obuf.at[t, m], rbuf.at[t, m - 1], m_s.at[t + 1, m], r_r.at[t, m - 1], at(3))
+
+    def pass_on(t, m):
+        return rc(rbuf.at[t, m - 1], msg.at[t + 1, m], r_s.at[t, m - 1], m_r.at[t + 1, m], at(-4))
+
+    def emit_last(members):
+        for m in members:
+            swap(obuf.at[ticks - 1, m], out.at[m], o_s.at[m], o_r.at[m])
+
+    def emit_early(t):
+        more = t < ticks - 1
+
+        @pl.when(jnp.logical_and(more, around))
+        def _():
+            for m in (1, 2):
+                send_around(t, m).start()
+
+        @pl.when(jnp.logical_and(more, lax.rem(sec, 4) > 0))
+        def _():
+            for m in (1, 2):
                 send_down(t, m).start()
 
-        @pl.when(t == ticks - 1)
-        def _():
-            for m in members:
-                swap(obuf.at[ticks - 1, m], out.at[m], o_s.at[m], o_r.at[m])
+        @pl.when(jnp.logical_not(more))
+        def _():
+            emit_last((1, 2))
+
+    def emit_late(t):
+        more = t < ticks - 1
+
+        @pl.when(jnp.logical_and(more, sec > 0))
+        def _():
+            for m in (3, 0):
+                send_down(t, m).start()
+
+        @pl.when(jnp.logical_not(more))
+        def _():
+            emit_last((3, 0))
+
+    def relay(t):
+        @pl.when(jnp.logical_and(t < ticks - 1, passes))
+        def _():
+            for m in (1, 2):
+                wait_for(rbuf.at[t, m - 1], r_r.at[t, m - 1])
+                pass_on(t, m).start()
 
     w = lax.broadcasted_iota(jnp.int32, (128, C), 0)
 
@@ -253,6 +293,7 @@
                 swap(fresh.at[t, m], msg.at[t + 1, m], w_s.at[t + 1, m], m_r.at[t + 1, m])
 
     V[:, :, 3 * c] = jnp.zeros((4, 3, 128, C), bf16)
+    gather_1(G, 0)
 
     def tick(t, carry):
         wait_for(msg.at[t, 3], m_r.at[t, 3])
@@ -262,13 +303,7 @@
             v = msg[t, 0, 128 * r:128 * r + 128].astype(f32)
             abuf[t, 0, 128 * r:128 * r + 128] = jax.nn.silu(v).astype(bf16)
         halo_send(t, 0, abuf.at[t, 0])
-        gather_1(G, t)
-
-        @pl.when(t > 0)
-        def _():
-            reduce_4(F, t - 1)
-            gather_0(F, t)
-
+        gather_2(G, t)
         for r in range(2):
             put(0, 1 + r, abuf[t, 0, 128 * r:128 * r + 128].astype(f32))
             put(1, 1 + r, msg[t, 3, 128 * r:128 * r + 128].astype(f32))
@@ -276,10 +311,15 @@
         halo_put(t, 0)
         kernel_grads(G, t, 0, msg[t, 3])
         reduce_0(G, t)
-        gather_1(F, t)
+
+        @pl.when(t > 0)
+        def _():
+            reduce_4(F, t - 1)
+            gather_0(F, t)
+
+        gather_3(G, t)
         reduce_1(G, t)
-        gather_2(G, t)
-        gather_3(G, t)
+        gather_4(G, t)
 
         wait_for(msg.at[t, 1], m_r.at[t, 1])
         prev_two = (msg[t, 1].astype(f32) - conv(G, t, 0)).astype(bf16)
@@ -291,8 +331,8 @@
                     + slope(msg[t, 0].astype(f32)) * conv_flip(G, t, 1)).astype(bf16)
         obuf[t, 2] = back_one
         halo_send(t, 3, obuf.at[t, 2])
-        emit(t, (1, 2))
-        gather_2(F, t)
+        emit_early(t)
+        gather_1(F, t)
         reduce_2(G, t)
         for r in range(2):
             put(2, 1 + r, abuf[t, 1, 128 * r:128 * r + 128].astype(f32))
@@ -301,19 +341,27 @@
         halo_put(t, 3)
         kernel_grads(F, t, 2, obuf[t, 2])
         reduce_0(F, t)
+        gather_2(F, t)
+        reduce_3(G, t)
+        reduce_1(F, t)
         gather_3(F, t)
+        reduce_4(G, t)
+
+        @pl.when(t < ticks - 1)
+        def _():
+            gather_0(G, t + 1)
+
+        gather_4(F, t)
         obuf[t, 0] = (msg[t, 0].astype(f32) - conv(F, t, 2)).astype(bf16)
         obuf[t, 3] = (msg[t, 3].astype(f32)
                       + slope(obuf[t, 1].astype(f32)) * conv_flip(F, t, 3)).astype(bf16)
-        emit(t, (3, 0))
-        reduce_1(F, t)
-        reduce_3(G, t)
+        emit_late(t)
         reduce_2(F, t)
-        reduce_4(G, t)
+        relay(t)
 
         @pl.when(t < ticks - 1)
         def _():
-            gather_0(G, t + 1)
+            gather_1(G, t + 1)
 
         reduce_3(F, t)
         gather_sent(G, t)
@@ -341,6 +389,12 @@
         for t in range(1, ticks):
             for m in range(4):
                 wait_for(out.at[m], w_s.at[t, m])
+
+    @pl.when(passes)
+    def _():
+        for t in range(ticks - 1):
+            for m in range(2):
+                wait_for(rbuf.at[t, m], r_s.at[t, m])
 
     @pl.when(sec > 0)
     def _():
@@ -368,6 +422,7 @@
             pltpu.VMEM((T, 4, cells, C), bf16),
             pltpu.VMEM((T, 4, cells, C), bf16),
             pltpu.VMEM((T, 2, cells, C), bf16),
+            pltpu.VMEM((T - 1, 2, cells, C), bf16),
             pltpu.VMEM((T, 4, 128, C), bf16),
             pltpu.VMEM((4, 3, 4, 128, C), bf16),
             pltpu.VMEM((2, T, 9, C, C), bf16),
@@ -378,7 +433,7 @@
             pltpu.VMEM((2, T, 9, C, C), bf16),
             dma((2, T, 15)), dma((2, T, 15)),
             dma((2, T, 11)), dma((2, T, 11)),
-            dma((T, 4)), dma((T, 4)), dma((T, 4)),
+            dma((T, 4)), dma((T, 4)), dma((T, 4)), dma((T - 1, 2)), dma((T - 1, 2)),
             dma((T, 4)), dma((T, 4)),
             dma((4,)), dma((4,)),
         ],

time: 188 us -> 150 us (0.80)
  Pallas kernels: 176 us -> 137 us
    pallas_call x1, Pallas kernels: 176 us -> 137 us  [local(): pl.pallas_call(kernel, out_shape=(jax.ShapeDtypeStruct((4, cells, C), bf1...]
where the time goes in v1:
time: 150 us; the launch traced here: 149 us
  Pallas kernels  137 us (91%)
  local copies, waits for them, and re-layouts  11.3 us (8%)
    pallas_call x1, Pallas kernels, local(): pl.pallas_call(kernel, out_shape=(jax.ShapeDtypeStruct((4, cells, C), bf1...  137 us
    transpose x1, local copies, waits for them, and re-layouts, local(): later = fresh[:, :, 0].transpose(0, 1, 3, 4, 2).reshape(T - 1, 4, cells, C)  4.84 us

profile of v1, /device:TPU:88, one launch (start us, length us, event | category | flops | bytes accessed | tf_op | source)
XLA Modules:
  0.0 149.2 jit_solution(17216052827186399518)
XLA Ops:
  0.6 2.0 %copy.7 = bf16[4,2,128,256]{3,2,1,0:T(8,128)(2,1)} copy(bf16[4,2,128,256]{2,1,3,0:T(2,128)(2,1)} %bitcast.18) | data formatting | bytes 1048576 | tf_op jit(solution)/shard_map/transpose | solution.py:410
  2.6 4.8 %copy.8 = bf16[3,4,2,128,256]{4,3,2,1,0:T(8,128)(2,1)} copy(bf16[3,4,2,128,256]{3,2,4,1,0:T(2,128)(2,1)} %bitcast.16) | data formatting | bytes 3145728 | tf_op jit(solution)/shard_map/transpose | solution.py:411
  7.4 137.3 %relay.1 = (bf16[4,256,256]{2,1,0:T(8,128)(2,1)}, f32[2,9,16,256]{3,2,1,0:T(8,128)}, f32[2,9,16,256]{3,2,1,0:T(8,128)}) custom-call(bf16[4,256,256]{2,1,0:T(8,128)(2,1)} %bitcast.21, bf16[3,4,256,256]{3,2,1,0:T(8,128)(2,1)} %bitcast.17, f32[2,9,16,256]{3,2,1,0:T(8,128)} %bitcast.24, f32[2,9,16,256]{3,2,1,0:T(8,128)} %bitcast.25), custom_call_target="tpu_custom_call" | custom-call | flops 7247757312 | bytes 4194304 | tf_op jit(solution)/shard_map/relay/pallas_call | solution.py:415
  144.8 0.0 copy-start
  144.8 2.0 %copy.9 = bf16[4,2,128,256]{2,1,3,0:T(2,128)(2,1)} copy(bf16[4,2,128,256]{3,2,1,0:T(8,128)(2,1)} %bitcast.20) | data formatting | bytes 1048576 | tf_op jit(solution)/shard_map/reshape | solution.py:446
  146.8 1.7 %copy.12 = f32[1,2,9,16,256]{4,3,2,1,0:T(8,128)} copy(f32[1,2,9,16,256]{4,3,2,1,0:T(8,128)} %bitcast.23) | data formatting | bytes 589824
  148.5 0.0 copy-done
  148.5 0.7 copy.13
Async XLA Ops:
  144.8 3.8 %copy-start = (f32[2,9,16,256]{3,2,1,0:T(8,128)S(1)}, f32[2,9,16,256]{3,2,1,0:T(8,128)}, u32[]{:S(2)}) copy-start(f32[2,9,16,256]{3,2,1,0:T(8,128)} %get-tuple-element.8) | copy-start | bytes 884740

commit v2 on v1

v2 whole, which is shorter than its diff:
```python
import math

import jax
import jax.numpy as jnp
from jax import lax
from jax.experimental import pallas as pl
from jax.experimental.pallas import tpu as pltpu
from jax.sharding import PartitionSpec as P

MESH = pl.DeviceIdType.MESH
LEARN_RATE = 0.05
MOMENTUM = 0.9
F, G = 0, 1
RS = ('zf', 'zf')
AG = ('dz', 'dz')
ORDER = ('MG', 'GR', 'A1F', 'A2G', 'R1G', 'A3G', 'CG', 'A2F', 'FR', 'R2G', 'R1F', 'A3F', 'RZG', 'A0G',
         'RE', 'CF', 'R2F', 'A1G', 'FU', 'RZF', 'A0F', 'SE')
bf16, f32 = jnp.bfloat16, jnp.float32


def wait_for(ref, sem):
    pltpu.make_async_copy(ref, ref, sem).wait()


def slope(v):
    s = jax.nn.sigmoid(v)
    return s * (1.0 + v * (1.0 - s))


def kernel(inbox, fresh, par_in, mom_in, out, par, mom, last,
           msg, obuf, abuf, rbuf, halo, V, gp, crecv, mrecv, fs, kbuf, first, later, final, wide,
           ag_s, ag_r, rs_s, rs_r, m_s, m_r, f_s, f_r, r_s, r_r, h_s, h_r, o_s, o_r):
    ticks = msg.shape[0]
    C = msg.shape[3]
    scale = 1.0 / math.sqrt(9 * C)
    sec = lax.axis_index("section")
    n_sec = lax.axis_size("section")
    dp = lax.axis_index("dp")
    z = lax.axis_index("spatial")
    x = dp // 2
    c = lax.rem(dp, 2)
    xp, xm, x2 = lax.rem(x + 1, 4), lax.rem(x + 3, 4), lax.rem(x + 2, 4)
    XP = {"dp": lax.rem(dp + 2, 8)}
    XM = {"dp": lax.rem(dp + 6, 8)}
    X2 = {"dp": lax.rem(dp + 4, 8)}
    CP = {"dp": dp + 1 - 2 * c}
    ZP = {"spatial": 1 - z}
    DG = {"dp": dp + 1 - 2 * c, "spatial": 1 - z}
    def far(dev):
        return {**dev, "spatial": 1 - z}

    def at(offset):
        return {"section": lax.rem(sec + n_sec + offset, n_sec)}

    around = jnp.logical_and(lax.rem(sec, 4) == 0, sec > 0)
    passes = jnp.logical_and(lax.rem(sec, 4) == 3, sec > 3)
    top = sec == n_sec - 1
    stays = c == z

    def rc(src, dst, ss, rs, dev):
        return pltpu.make_async_remote_copy(
            src_ref=src, dst_ref=dst, send_sem=ss, recv_sem=rs,
            device_id=dev, device_id_type=MESH)

    barrier = pltpu.get_barrier_semaphore()
    for dev in (XP, XM, X2, CP, ZP, DG, far(XP), far(XM), far(X2), at(1), at(-1), at(3), at(-3), at(4), at(-4)):
        pl.semaphore_signal(barrier, inc=1, device_id=dev, device_id_type=MESH)
    pl.semaphore_wait(barrier, 15)

    def row(xx, cc, zz):
        return pl.multiple_of(64 * xx + 32 * cc + 16 * zz, 16)

    def kpart(k, t, xx, zz):
        return kbuf.at[k, t, :, pl.ds(row(xx, c, zz), 16), :]

    def ag(k, t, i, xx, zz, dev):
        part = kpart(k, t, xx, zz)
        return rc(part, part, ag_s.at[k, t, i], ag_r.at[k, t, i], dev)

    def ag_to(k, t, zz):
        ways = [ag(k, t, 5 + zz, x, zz, XP), ag(k, t, 1 + zz, x, zz, XM)]
        if AG[k] == 'dz':
            ways.append(ag(k, t, 3 + zz, x, zz, X2))
        return ways + [ag(k, t, 13 + zz, x, zz, CP)]

    def ag_wait(k, t, i):
        wait_for(kpart(k, t, x, z), ag_r.at[k, t, i])

    def gather_0(k, t):
        kbuf[k, t, :, pl.ds(row(x, c, z), 16), :] = (par[k] * scale).astype(bf16)
        ag(k, t, 0, x, z, ZP).start()
        for d in ag_to(k, t, z):
            d.start()

    def gather_1(k, t):
        ag_wait(k, t, 0)
        for d in ag_to(k, t, 1 - z):
            d.start()

    def hand_over(k, t, zz):
        for d, xx in ((0, xp), (2, xm), (1, x2)):
            ag_wait(k, t, 1 + 2 * d + zz)
            ag(k, t, 7 + 2 * d + zz, xx, zz, CP).start()

    def gather_2(k, t):
        if AG[k] == 'dz':
            hand_over(k, t, z)
            return
        ag_wait(k, t, 5)
        ag(k, t, 3, xm, 0, XP).start()
        ag(k, t, 11, xm, 0, CP).start()
        ag_wait(k, t, 2)
        ag(k, t, 4, xp, 1, XM).start()
        ag(k, t, 8, xp, 1, CP).start()
        ag_wait(k, t, 6)
        ag(k, t, 12, xm, 1, CP).start()
        ag_wait(k, t, 1)
        ag(k, t, 7, xp, 0, CP).start()

    def gather_3(k, t):
        if AG[k] == 'dz':
            hand_over(k, t, 1 - z)
            return
        for zz in range(2):
            ag_wait(k, t, 3 + zz)
            ag(k, t, 9 + zz, x2, zz, CP).start()

    def gather_4(k, t):
        for i in range(7, 15):
            ag_wait(k, t, i)

    def gather_sent(k, t):
        for i in range(15):
            wait_for(kpart(k, t, x, z), ag_s.at[k, t, i])

    def gpart(k, t, xx, zz):
        return gp.at[k, t, :, pl.ds(row(xx, c, zz), 16), :]

    order = (x2, xp, xm, x)

    def reduce_0(k, t):
        for j in range(4):
            rc(gp.at[k, t, :, pl.ds(row(order[j], 1 - c, 0), 32), :],
               crecv.at[k, t, :, pl.ds(pl.multiple_of(32 * order[j], 32), 32), :],
               rs_s.at[k, t, j], rs_r.at[k, t, j], CP).start()

    def part_to(k, t, m, xx, zz, dev):
        return rc(gpart(k, t, xx, zz), mrecv.at[k, t, m], rs_s.at[k, t, 4 + m], rs_r.at[k, t, 4 + m], dev)

    def part_wait(k, t, m):
        wait_for(mrecv.at[k, t, m], rs_r.at[k, t, 4 + m])

    def part_add(k, t, m, xx, zz):
        part_wait(k, t, m)
        mine = gpart(k, t, xx, zz)
        mine[...] = (mine[...].astype(f32) + mrecv[k, t, m].astype(f32)).astype(bf16)

    def reduce_1(k, t):
        for j in range(4):
            xx = order[j]
            other = crecv.at[k, t, :, pl.ds(pl.multiple_of(32 * xx, 32), 32), :]
            wait_for(other, rs_r.at[k, t, j])
            mine = gp.at[k, t, :, pl.ds(row(xx, c, 0), 32), :]
            mine[...] = (mine[...].astype(f32) + other[...].astype(f32)).astype(bf16)
            dev = (X2, XP, XM, None)[j]
            m = (2, 0, 1, 6)[j]
            if RS[k] == 'zf':
                part_to(k, t, j, xx, 1 - z, ZP).start()
            elif RS[k] == 'cur':
                if j == 0:
                    part_to(k, t, 0, xx, 0, XP).start()
                    part_to(k, t, 3, xx, 1, XM).start()
                elif j == 1:
                    part_to(k, t, 1, xx, 1, XP).start()
                elif j == 2:
                    part_to(k, t, 4, xx, 0, XM).start()
            elif dev is None:
                part_to(k, t, 6, xx, 1 - z, ZP).start()
            else:
                part_to(k, t, m + 3, xx, 1 - z, far(dev)).start()
                part_to(k, t, m, xx, z, dev).start()

    def reduce_2(k, t):
        if RS[k] == 'zf':
            for j in range(4):
                part_add(k, t, j, order[j], z)
                if j < 3:
                    part_to(k, t, 4 + j, order[j], z, (X2, XP, XM)[j]).start()
        if RS[k] == 'cur':
            part_add(k, t, 0, xp, 0)
            part_to(k, t, 2, xp, 0, XP).start()
            part_add(k, t, 3, xm, 1)
            part_to(k, t, 5, xm, 1, XM).start()

    def reduce_3(k, t):
        if RS[k] == 'cur':
            for m in (1, 4, 2, 5):
                part_wait(k, t, m)

            def total(zz):
                return (gpart(k, t, x, zz)[...].astype(f32)
                        + mrecv[k, t, 2 - zz].astype(f32) + mrecv[k, t, 4 + zz].astype(f32))

            theirs = gpart(k, t, x, 1 - z)
            theirs[...] = total(1 - z).astype(bf16)
            part_to(k, t, 6, x, 1 - z, ZP).start()
            fs[k] = total(z)

    def update(k, t):
        late = {'zf': (4, 5, 6), 'cur': (6,), 'direct': range(7)}[RS[k]]
        grad = fs[k] if RS[k] == 'cur' else gpart(k, t, x, z)[...].astype(f32)
        for m in late:
            part_wait(k, t, m)
        for m in late:
            grad = grad + mrecv[k, t, m].astype(f32)
        @pl.when(t < ticks - 1)
        def _():
            mom[k] = MOMENTUM * mom[k] + scale * grad
            par[k] = par[k] - LEARN_RATE * mom[k]

        @pl.when(t == ticks - 1)
        def _():
            last[k] = grad

    def reduce_sent(k, t):
        for j in range(4):
            wait_for(crecv.at[k, t, :, pl.ds(0, 32), :], rs_s.at[k, t, j])
        for i in range(4, 11):
            wait_for(mrecv.at[k, t, 0], rs_s.at[k, t, i])

    def swap(src, dst, ss, rs):
        @pl.when(stays)
        def _():
            pltpu.make_async_copy(src, dst, rs).start()

        @pl.when(jnp.logical_not(stays))
        def _():
            rc(src, dst, ss, rs, DG).start()

    def send_down(t, m):
        return rc(obuf.at[t, m], msg.at[t + 1, m], m_s.at[t + 1, m], m_r.at[t + 1, m], at(-1))

    def send_around(t, m):
        return rc(obuf.at[t, m], rbuf.at[t, m - 1], m_s.at[t + 1, m], r_r.at[t, m - 1], at(3))

    def pass_on(t, m):
        return rc(rbuf.at[t, m - 1], msg.at[t + 1, m], r_s.at[t, m - 1], m_r.at[t + 1, m], at(-4))

    def emit_last(members):
        for m in members:
            pack(obuf.at[ticks - 1, m], final.at[m])
            swap(final.at[m], out.at[m], o_s.at[m], o_r.at[m])

    def emit_early(t):
        more = t < ticks - 1

        @pl.when(jnp.logical_and(more, around))
        def _():
            for m in (1, 2):
                send_around(t, m).start()

        @pl.when(jnp.logical_and(more, lax.rem(sec, 4) > 0))
        def _():
            for m in (1, 2):
                send_down(t, m).start()

        @pl.when(jnp.logical_not(more))
        def _():
            emit_last((1, 2))

    def emit_late(t):
        more = t < ticks - 1

        @pl.when(jnp.logical_and(more, sec > 0))
        def _():
            for m in (3, 0):
                send_down(t, m).start()

        @pl.when(jnp.logical_not(more))
        def _():
            emit_last((3, 0))

    def relay(t):
        @pl.when(jnp.logical_and(t < ticks - 1, passes))
        def _():
            for m in (1, 2):
                wait_for(rbuf.at[t, m - 1], r_r.at[t, m - 1])
                pass_on(t, m).start()

    def unpack(src, dst):
        wide[...] = src[...].astype(f32)
        for r in range(2):
            dst[128 * r:128 * r + 128] = wide[pl.ds(r, C, stride=2), :].T.astype(bf16)

    def pack(src, dst):
        for r in range(2):
            wide[pl.ds(r, C, stride=2), :] = src[128 * r:128 * r + 128].astype(f32).T
        dst[...] = wide[...].astype(bf16)

    def msg_wait(t, m):
        @pl.when(jnp.logical_and(t > 0, jnp.logical_not(top)))
        def _():
            wait_for(msg.at[t, m], m_r.at[t, m])

    def take_fresh(t):
        @pl.when(jnp.logical_and(t < ticks - 1, top))
        def _():
            for m in (3, 0, 1, 2):
                wait_for(later.at[t, m], f_r.at[t + 1, m])
                unpack(later.at[t, m], msg.at[t + 1, m])

    w = lax.broadcasted_iota(jnp.int32, (128, C), 0)

    def put(f, r, v):
        V[f, 1, r] = v.astype(bf16)
        V[f, 0, r] = jnp.where(w == 0, 0.0, pltpu.roll(v, 1, 0)).astype(bf16)
        V[f, 2, r] = jnp.where(w == 127, 0.0, pltpu.roll(v, 127, 0)).astype(bf16)

    def window(f, a, b):
        return V[f, b, a:a + 2].reshape(256, C)

    hoff = pl.multiple_of(128 * (1 - c), 128)
    hrow = 3 * (1 - c)

    def halo_send(t, f, src):
        rc(src.at[pl.ds(hoff, 128), :], halo.at[t, f], h_s.at[t, f], h_r.at[t, f], CP).start()

    def halo_put(t, f):
        wait_for(halo.at[t, f], h_r.at[t, f])
        put(f, hrow, halo[t, f].astype(f32))

    def kernel_grads(k, t, fa, g):
        gt = g.T
        for a in range(3):
            for b in range(3):
                gp[k, t, 3 * a + b] = jnp.dot(
                    gt, window(fa, a, b), preferred_element_type=f32).astype(bf16)

    def conv(k, t, f):
        acc = jnp.zeros((256, C), f32)
        for a in range(3):
            for b in range(3):
                acc = acc + lax.dot_general(
                    window(f, a, b), kbuf[k, t, 3 * a + b], (((1,), (1,)), ((), ())),
                    preferred_element_type=f32)
        return acc

    def conv_flip(k, t, f):
        acc = jnp.zeros((256, C), f32)
        for a in range(3):
            for b in range(3):
                acc = acc + jnp.dot(
                    window(f, 2 - a, 2 - b), kbuf[k, t, 3 * a + b], preferred_element_type=f32)
        return acc

    par[...] = par_in[...]
    mom[...] = mom_in[...]
    gather_0(G, 0)
    for m in (3, 0, 1, 2):
        swap(inbox.at[m], first.at[m], f_s.at[0, m], f_r.at[0, m])
    gather_0(F, 0)

    @pl.when(top)
    def _():
        for t in range(ticks - 1):
            for m in (3, 0, 1, 2):
                swap(fresh.at[t, m], later.at[t, m], f_s.at[t + 1, m], f_r.at[t + 1, m])

    V[:, :, 3 * c] = jnp.zeros((4, 3, 128, C), bf16)
    def open_first(m):
        wait_for(first.at[m], f_r.at[0, m])
        unpack(first.at[m], msg.at[0, m])

    open_first(3)
    open_first(0)
    for k, name in ((G, 'A1G'), (F, 'A1F')):
        if name not in ORDER[:ORDER.index('C' + name[-1])]:
            gather_1(k, 0)
    open_first(1)
    open_first(2)

    def begin(t):
        msg_wait(t, 3)
        halo_send(t, 1, msg.at[t, 3])
        msg_wait(t, 0)
        for r in range(2):
            v = msg[t, 0, 128 * r:128 * r + 128].astype(f32)
            abuf[t, 0, 128 * r:128 * r + 128] = jax.nn.silu(v).astype(bf16)
        halo_send(t, 0, abuf.at[t, 0])
        for r in range(2):
            put(0, 1 + r, abuf[t, 0, 128 * r:128 * r + 128].astype(f32))
            put(1, 1 + r, msg[t, 3, 128 * r:128 * r + 128].astype(f32))

    def grads_g(t):
        halo_put(t, 1)
        halo_put(t, 0)
        kernel_grads(G, t, 0, msg[t, 3])
        reduce_0(G, t)

    def convs_g(t):
        gather_4(G, t)
        msg_wait(t, 1)
        prev_two = (msg[t, 1].astype(f32) - conv(G, t, 0)).astype(bf16)
        obuf[t, 1] = prev_two
        abuf[t, 1] = jax.nn.silu(prev_two.astype(f32)).astype(bf16)
        halo_send(t, 2, abuf.at[t, 1])
        msg_wait(t, 2)
        back_one = (msg[t, 2].astype(f32)
                    + slope(msg[t, 0].astype(f32)) * conv_flip(G, t, 1)).astype(bf16)
        obuf[t, 2] = back_one
        halo_send(t, 3, obuf.at[t, 2])
        emit_early(t)
        for r in range(2):
            put(2, 1 + r, abuf[t, 1, 128 * r:128 * r + 128].astype(f32))
            put(3, 1 + r, obuf[t, 2, 128 * r:128 * r + 128].astype(f32))

    def grads_f(t):
        halo_put(t, 2)
        halo_put(t, 3)
        kernel_grads(F, t, 2, obuf[t, 2])
        reduce_0(F, t)

    def convs_f(t):
        gather_4(F, t)
        obuf[t, 0] = (msg[t, 0].astype(f32) - conv(F, t, 2)).astype(bf16)
        obuf[t, 3] = (msg[t, 3].astype(f32)
                      + slope(obuf[t, 1].astype(f32)) * conv_flip(F, t, 3)).astype(bf16)
        emit_late(t)

    def sent(t):
        gather_sent(G, t)
        gather_sent(F, t)
        reduce_sent(G, t)
        reduce_sent(F, t)
        for f in range(4):
            wait_for(halo.at[t, f], h_s.at[t, f])

    def step(name, t):
        k = G if name[-1] == 'G' else F
        plain = {'MG': begin, 'GR': grads_g, 'CG': convs_g, 'FR': grads_f, 'CF': convs_f,
                 'RE': relay, 'FU': take_fresh, 'SE': sent}
        if name in plain:
            plain[name](t)
            return
        stage = {'A0': gather_0, 'A1': gather_1, 'A2': gather_2, 'A3': gather_3,
                 'R1': reduce_1, 'R2': reduce_2, 'R3': reduce_3, 'RZ': update}[name[:2]]
        if name[:2] in ('A0', 'A1') and name not in ORDER[:ORDER.index('C' + name[-1])]:
            @pl.when(t < ticks - 1)
            def _():
                stage(k, t + 1)
        else:
            stage(k, t)

    def tick(t, carry):
        for name in ORDER:
            step(name, t)
        return carry

    lax.fori_loop(0, ticks, tick, 0)
    for m in range(4):
        wait_for(out.at[m], o_r.at[m])

    @pl.when(jnp.logical_not(stays))
    def _():
        for m in range(4):
            wait_for(out.at[m], o_s.at[m])
            wait_for(out.at[m], f_s.at[0, m])

    @pl.when(jnp.logical_and(top, jnp.logical_not(stays)))
    def _():
        for t in range(1, ticks):
            for m in range(4):
                wait_for(out.at[m], f_s.at[t, m])

    @pl.when(passes)
    def _():
        for t in range(ticks - 1):
            for m in range(2):
                wait_for(rbuf.at[t, m], r_s.at[t, m])

    @pl.when(sec > 0)
    def _():
        for t in range(1, ticks):
            for m in range(4):
                wait_for(out.at[m], m_s.at[t, m])


def local(inbox, fresh, params, moments):
    T = fresh.shape[0] + 1
    C = inbox.shape[3]
    cells = inbox.shape[4] * inbox.shape[5]
    raw = (C * inbox.shape[4], inbox.shape[5])
    mine = inbox.reshape(4, *raw)
    later = fresh.reshape(T - 1, 4, *raw)
    shard = params.shape[1:]
    vmem = pl.BlockSpec(memory_space=pltpu.VMEM)
    dma = pltpu.SemaphoreType.DMA
    out, par, mom, grad = pl.pallas_call(
        kernel,
        out_shape=(jax.ShapeDtypeStruct((4, *raw), bf16),) + (jax.ShapeDtypeStruct(shard, f32),) * 3,
        in_specs=[vmem, pl.BlockSpec(memory_space=pl.ANY), vmem, vmem],
        out_specs=(vmem,) * 4,
        scratch_shapes=[
            pltpu.VMEM((T, 4, cells, C), bf16),
            pltpu.VMEM((T, 4, cells, C), bf16),
            pltpu.VMEM((T, 2, cells, C), bf16),
            pltpu.VMEM((T - 1, 2, cells, C), bf16),
            pltpu.VMEM((T, 4, 128, C), bf16),
            pltpu.VMEM((4, 3, 4, 128, C), bf16),
            pltpu.VMEM((2, T, 9, C, C), bf16),
            pltpu.VMEM((2, T, 9, C // 2, C), bf16),
            pltpu.VMEM((2, T, 7, 9, 16, C), bf16),
            pltpu.VMEM((2, 9, 16, C), f32),
            pltpu.VMEM((2, T, 9, C, C), bf16),
            pltpu.VMEM((4, *raw), bf16),
            pltpu.VMEM((T - 1, 4, *raw), bf16),
            pltpu.VMEM((4, *raw), bf16),
            pltpu.VMEM(raw, f32),
            dma((2, T, 15)), dma((2, T, 15)),
            dma((2, T, 11)), dma((2, T, 11)),
            dma((T, 4)), dma((T, 4)), dma((T, 4)), dma((T, 4)), dma((T - 1, 2)), dma((T - 1, 2)),
            dma((T, 4)), dma((T, 4)),
            dma((4,)), dma((4,)),
        ],
        compiler_params=pltpu.CompilerParams(
            collective_id=0, has_side_effects=True, vmem_limit_bytes=60 << 20),
        cost_estimate=pl.CostEstimate(
            flops=T * 6 * 9 * 2 * C * C * cells, bytes_accessed=1 << 22, transcendentals=0),
        name="relay",
    )(mine, later, params[0], moments[0])
    mom = MOMENTUM * mom + grad / math.sqrt(9 * C)
    par = par - LEARN_RATE * mom
    return (out.reshape(inbox.shape), par[None], mom[None])


def solution(mesh):
    cells = P("section", None, "dp", None, "spatial", None)
    shards = P("section", None, None, ("dp", "spatial"), None)
    return jax.shard_map(
        local,
        mesh=mesh,
        in_specs=(cells, P(None, None, "dp", None, "spatial", None), shards, shards),
        out_specs=(cells, shards, shards),
        check_vma=False,
    )
```

time: 150 us -> 142 us (0.947)
  local copies, waits for them, and re-layouts: 11.3 us -> 0.8 us
  other arithmetic: 0 us -> 2.1 us
    transpose x2 -> x0, local copies, waits for them, and re-layouts: 6.8 us -> none  [the longest x1 4.84 us: local(): later = fresh[:, :, 0].transpose(0, 1, 3, 4, 2).reshape(T - 1, 4, cells, C)]
    broadcast_in_dim x0 -> x1, other arithmetic: none -> 2.1 us  [local(): return (out.reshape(inbox.shape), par[None], mom[None])]
    reshape x1 -> x0, local copies, waits for them, and re-layouts: 2.05 us -> none  [local(): out.reshape(4, *inbox.shape[4:], C).transpose(0, 3, 1, 2)[None, :, None]]
    unnamed x4 -> x3, local copies, waits for them, and re-layouts: 2.41 us -> 0.8 us
where the time goes in v2:
time: 142 us; the launch traced here: 140 us
  Pallas kernels  137 us (96%)
  other arithmetic  2.1 us (1%)
    pallas_call x1, Pallas kernels, local(): pl.pallas_call(kernel, out_shape=(jax.ShapeDtypeStruct((4, *raw), bf16),)...  137 us

profile of v2, /device:TPU:88, one launch (start us, length us, event | category | flops | bytes accessed | tf_op | source)
XLA Modules:
  0.0 140.1 jit_solution(241270684744464791)
XLA Ops:
  0.6 136.6 %relay.1 = (bf16[4,512,128]{2,1,0:T(8,128)(2,1)}, f32[2,9,16,256]{3,2,1,0:T(8,128)}, f32[2,9,16,256]{3,2,1,0:T(8,128)}, f32[2,9,16,256]{3,2,1,0:T(8,128)}) custom-call(bf16[4,512,128]{2,1,0:T(8,128)(2,1)} %bitcast.13, bf16[3,4,512,128]{3,2,1,0:T(8,128)(2,1)} %bitcast.12, f32[2,9,16,256]{3,2,1,0:T(8,128)} %bitcast.14, f32[2,9,16,256]{3,2,1,0:T(8,128)} %bitcast.15), custom_call_target="tpu_custom_call" | custom-call | flops 7247757312 | bytes 4194304 | tf_op jit(solution)/shard_map/relay/pallas_call | solution.py:498
  137.2 0.0 copy-start
  137.2 2.1 %fusion = (f32[1,2,9,16,256]{4,3,2,1,0:T(8,128)}, f32[1,2,9,16,256]{4,3,2,1,0:T(8,128)}) fusion(f32[2,9,16,256]{3,2,1,0:T(8,128)} %get-tuple-element.10, f32[2,9,16,256]{3,2,1,0:T(8,128)} %get-tuple-element.9, f32[2,9,16,256]{3,2,1,0:T(8,128)} %get-tuple-element.8), kind=kLoop, calls=%fused_computation.2 | loop fusion | flops 368640 | bytes 1474560 | tf_op jit(solution)/shard_map/broadcast_in_dim | solution.py:533
  139.3 0.0 copy-done
  139.3 0.8 copy.9
Async XLA Ops:
  137.2 2.1 %copy-start = (bf16[4,512,128]{2,1,0:T(8,128)(2,1)S(1)}, bf16[4,512,128]{2,1,0:T(8,128)(2,1)}, u32[]{:S(2)}) copy-start(bf16[4,512,128]{2,1,0:T(8,128)(2,1)} %get-tuple-element.7) | copy-start | bytes 1572868

commit v3 on v2

--- a/solution.py
+++ b/solution.py
@@ -11,7 +11,7 @@
 LEARN_RATE = 0.05
 MOMENTUM = 0.9
 F, G = 0, 1
-RS = ('zf', 'zf')
+RS = ('xf', 'zf')
 AG = ('dz', 'dz')
 ORDER = ('MG', 'GR', 'A1F', 'A2G', 'R1G', 'A3G', 'CG', 'A2F', 'FR', 'R2G', 'R1F', 'A3F', 'RZG', 'A0G',
          'RE', 'CF', 'R2F', 'A1G', 'FU', 'RZF', 'A0F', 'SE')
@@ -166,6 +166,10 @@
             m = (2, 0, 1, 6)[j]
             if RS[k] == 'zf':
                 part_to(k, t, j, xx, 1 - z, ZP).start()
+            elif RS[k] == 'xf':
+                for zz in range(2):
+                    if j < 3:
+                        part_to(k, t, 2 * j + zz, xx, zz, dev).start()
             elif RS[k] == 'cur':
                 if j == 0:
                     part_to(k, t, 0, xx, 0, XP).start()
@@ -192,6 +196,21 @@
             part_add(k, t, 3, xm, 1)
             part_to(k, t, 5, xm, 1, XM).start()
 
+        if RS[k] == 'xf':
+            for m in (2, 3, 4, 5, 0, 1):
+                part_wait(k, t, m)
+
+            def total(zz):
+                grad = gpart(k, t, x, zz)[...].astype(f32)
+                for j in range(3):
+                    grad = grad + mrecv[k, t, 2 * j + zz].astype(f32)
+                return grad
+
+            theirs = gpart(k, t, x, 1 - z)
+            theirs[...] = total(1 - z).astype(bf16)
+            part_to(k, t, 6, x, 1 - z, ZP).start()
+            fs[k] = total(z)
+
     def reduce_3(k, t):
         if RS[k] == 'cur':
             for m in (1, 4, 2, 5):
@@ -207,8 +226,8 @@
             fs[k] = total(z)
 
     def update(k, t):
-        late = {'zf': (4, 5, 6), 'cur': (6,), 'direct': range(7)}[RS[k]]
-        grad = fs[k] if RS[k] == 'cur' else gpart(k, t, x, z)[...].astype(f32)
+        late = {'zf': (4, 5, 6), 'cur': (6,), 'xf': (6,), 'direct': range(7)}[RS[k]]
+        grad = fs[k] if RS[k] in ('cur', 'xf') else gpart(k, t, x, z)[...].astype(f32)
         for m in late:
             part_wait(k, t, m)
         for m in late:
@@ -268,17 +287,16 @@
         def _():
             emit_last((1, 2))
 
-    def emit_late(t):
+    def emit_late(t, m):
         more = t < ticks - 1
 
         @pl.when(jnp.logical_and(more, sec > 0))
         def _():
-            for m in (3, 0):
-                send_down(t, m).start()
+            send_down(t, m).start()
 
         @pl.when(jnp.logical_not(more))
         def _():
-            emit_last((3, 0))
+            emit_last((m,))
 
     def relay(t):
         @pl.when(jnp.logical_and(t < ticks - 1, passes))
@@ -358,6 +376,12 @@
     gather_0(G, 0)
     for m in (3, 0, 1, 2):
         swap(inbox.at[m], first.at[m], f_s.at[0, m], f_r.at[0, m])
+    V[:, :, 3 * c] = jnp.zeros((4, 3, 128, C), bf16)
+    def open_first(m):
+        wait_for(first.at[m], f_r.at[0, m])
+        unpack(first.at[m], msg.at[0, m])
+
+    gather_1(G, 0)
     gather_0(F, 0)
 
     @pl.when(top)
@@ -366,16 +390,8 @@
             for m in (3, 0, 1, 2):
                 swap(fresh.at[t, m], later.at[t, m], f_s.at[t + 1, m], f_r.at[t + 1, m])
 
-    V[:, :, 3 * c] = jnp.zeros((4, 3, 128, C), bf16)
-    def open_first(m):
-        wait_for(first.at[m], f_r.at[0, m])
-        unpack(first.at[m], msg.at[0, m])
-
     open_first(3)
     open_first(0)
-    for k, name in ((G, 'A1G'), (F, 'A1F')):
-        if name not in ORDER[:ORDER.index('C' + name[-1])]:
-            gather_1(k, 0)
     open_first(1)
     open_first(2)
 
@@ -422,10 +438,11 @@
 
     def convs_f(t):
         gather_4(F, t)
-        obuf[t, 0] = (msg[t, 0].astype(f32) - conv(F, t, 2)).astype(bf16)
         obuf[t, 3] = (msg[t, 3].astype(f32)
                       + slope(obuf[t, 1].astype(f32)) * conv_flip(F, t, 3)).astype(bf16)
-        emit_late(t)
+        emit_late(t, 3)
+        obuf[t, 0] = (msg[t, 0].astype(f32) - conv(F, t, 2)).astype(bf16)
+        emit_late(t, 0)
 
     def sent(t):
         gather_sent(G, t)

time: 142 us -> 140 us (0.986)
  no operation moved by 1% of the time
where the time goes in v3:
time: 140 us; the launch traced here: 139 us
  Pallas kernels  136 us (97%)
  other arithmetic  2.1 us (2%)
    pallas_call x1, Pallas kernels, local(): pl.pallas_call(kernel, out_shape=(jax.ShapeDtypeStruct((4, *raw), bf16),)...  136 us

profile of v3, /device:TPU:88, one launch (start us, length us, event | category | flops | bytes accessed | tf_op | source)
XLA Modules:
  0.0 139.5 jit_solution(167630989244786758)
XLA Ops:
  0.6 135.9 %relay.1 = (bf16[4,512,128]{2,1,0:T(8,128)(2,1)}, f32[2,9,16,256]{3,2,1,0:T(8,128)}, f32[2,9,16,256]{3,2,1,0:T(8,128)}, f32[2,9,16,256]{3,2,1,0:T(8,128)}) custom-call(bf16[4,512,128]{2,1,0:T(8,128)(2,1)} %bitcast.13, bf16[3,4,512,128]{3,2,1,0:T(8,128)(2,1)} %bitcast.12, f32[2,9,16,256]{3,2,1,0:T(8,128)} %bitcast.14, f32[2,9,16,256]{3,2,1,0:T(8,128)} %bitcast.15), custom_call_target="tpu_custom_call" | custom-call | flops 7247757312 | bytes 4194304 | tf_op jit(solution)/shard_map/relay/pallas_call | solution.py:515
  136.6 0.0 copy-start
  136.6 2.1 %fusion = (f32[1,2,9,16,256]{4,3,2,1,0:T(8,128)}, f32[1,2,9,16,256]{4,3,2,1,0:T(8,128)}) fusion(f32[2,9,16,256]{3,2,1,0:T(8,128)} %get-tuple-element.10, f32[2,9,16,256]{3,2,1,0:T(8,128)} %get-tuple-element.9, f32[2,9,16,256]{3,2,1,0:T(8,128)} %get-tuple-element.8), kind=kLoop, calls=%fused_computation.2 | loop fusion | flops 368640 | bytes 1474560 | tf_op jit(solution)/shard_map/broadcast_in_dim | solution.py:550
  138.7 0.0 copy-done
  138.7 0.8 copy.9
Async XLA Ops:
  136.6 2.1 %copy-start = (bf16[4,512,128]{2,1,0:T(8,128)(2,1)S(1)}, bf16[4,512,128]{2,1,0:T(8,128)(2,1)}, u32[]{:S(2)}) copy-start(bf16[4,512,128]{2,1,0:T(8,128)(2,1)} %get-tuple-element.7) | copy-start | bytes 1572868

commit v4 on v3

--- a/solution.py
+++ b/solution.py
@@ -14,7 +14,7 @@
 RS = ('xf', 'zf')
 AG = ('dz', 'dz')
 ORDER = ('MG', 'GR', 'A1F', 'A2G', 'R1G', 'A3G', 'CG', 'A2F', 'FR', 'R2G', 'R1F', 'A3F', 'RZG', 'A0G',
-         'RE', 'CF', 'R2F', 'A1G', 'FU', 'RZF', 'A0F', 'SE')
+         'RE', 'CF', 'SB', 'R2F', 'A1G', 'FU', 'RZF', 'A0F', 'SE')
 bf16, f32 = jnp.bfloat16, jnp.float32
 
 
@@ -63,9 +63,9 @@
             device_id=dev, device_id_type=MESH)
 
     barrier = pltpu.get_barrier_semaphore()
-    for dev in (XP, XM, X2, CP, ZP, DG, far(XP), far(XM), far(X2), at(1), at(-1), at(3), at(-3), at(4), at(-4)):
+    for dev in (XP, XM, X2, CP, ZP, DG, at(1), at(-1), at(3), at(-3), at(4), at(-4)):
         pl.semaphore_signal(barrier, inc=1, device_id=dev, device_id_type=MESH)
-    pl.semaphore_wait(barrier, 15)
+    pl.semaphore_wait(barrier, 12)
 
     def row(xx, cc, zz):
         return pl.multiple_of(64 * xx + 32 * cc + 16 * zz, 16)
@@ -444,18 +444,20 @@
         obuf[t, 0] = (msg[t, 0].astype(f32) - conv(F, t, 2)).astype(bf16)
         emit_late(t, 0)
 
-    def sent(t):
+    def sent_before(t):
         gather_sent(G, t)
         gather_sent(F, t)
         reduce_sent(G, t)
-        reduce_sent(F, t)
         for f in range(4):
             wait_for(halo.at[t, f], h_s.at[t, f])
+
+    def sent(t):
+        reduce_sent(F, t)
 
     def step(name, t):
         k = G if name[-1] == 'G' else F
         plain = {'MG': begin, 'GR': grads_g, 'CG': convs_g, 'FR': grads_f, 'CF': convs_f,
-                 'RE': relay, 'FU': take_fresh, 'SE': sent}
+                 'RE': relay, 'FU': take_fresh, 'SE': sent, 'SB': sent_before}
         if name in plain:
             plain[name](t)
             return

time: 140 us -> 140 us (level)
  no operation moved by 1% of the time
where the time goes in v4:
time: 140 us; the launch traced here: 139 us
  Pallas kernels  136 us (97%)
  other arithmetic  2.1 us (2%)
    pallas_call x1, Pallas kernels, local(): pl.pallas_call(kernel, out_shape=(jax.ShapeDtypeStruct((4, *raw), bf16),)...  136 us

profile of v4, /device:TPU:88, one launch (start us, length us, event | category | flops | bytes accessed | tf_op | source)
XLA Modules:
  0.0 139.3 jit_solution(7391144692005902800)
XLA Ops:
  0.6 135.7 %relay.1 = (bf16[4,512,128]{2,1,0:T(8,128)(2,1)}, f32[2,9,16,256]{3,2,1,0:T(8,128)}, f32[2,9,16,256]{3,2,1,0:T(8,128)}, f32[2,9,16,256]{3,2,1,0:T(8,128)}) custom-call(bf16[4,512,128]{2,1,0:T(8,128)(2,1)} %bitcast.13, bf16[3,4,512,128]{3,2,1,0:T(8,128)(2,1)} %bitcast.12, f32[2,9,16,256]{3,2,1,0:T(8,128)} %bitcast.14, f32[2,9,16,256]{3,2,1,0:T(8,128)} %bitcast.15), custom_call_target="tpu_custom_call" | custom-call | flops 7247757312 | bytes 4194304 | tf_op jit(solution)/shard_map/relay/pallas_call | solution.py:517
  136.4 0.0 copy-start
  136.4 2.1 %fusion = (f32[1,2,9,16,256]{4,3,2,1,0:T(8,128)}, f32[1,2,9,16,256]{4,3,2,1,0:T(8,128)}) fusion(f32[2,9,16,256]{3,2,1,0:T(8,128)} %get-tuple-element.10, f32[2,9,16,256]{3,2,1,0:T(8,128)} %get-tuple-element.9, f32[2,9,16,256]{3,2,1,0:T(8,128)} %get-tuple-element.8), kind=kLoop, calls=%fused_computation.2 | loop fusion | flops 368640 | bytes 1474560 | tf_op jit(solution)/shard_map/broadcast_in_dim | solution.py:552
  138.5 0.0 copy-done
  138.5 0.8 copy.9
Async XLA Ops:
  136.4 2.1 %copy-start = (bf16[4,512,128]{2,1,0:T(8,128)(2,1)S(1)}, bf16[4,512,128]{2,1,0:T(8,128)(2,1)}, u32[]{:S(2)}) copy-start(bf16[4,512,128]{2,1,0:T(8,128)(2,1)} %get-tuple-element.7) | copy-start | bytes 1572868
